TPU v7x, 256 devices: a whole 4x4x8 slice. The times are simulated.
256 devices in a mesh: grp: 8 (over z), own: 32 (over y, x, core).
Axes of the slice: x: 4, y: 4, z: 8, core: 2. Of those that a mesh axis runs over, the one named last changes fastest.
Arguments:
- embeddings: bfloat16 [262144, 1024], P(('grp', 'own')), may hold values from -6 to 6
- assign_one: int32 [262144], P(('grp', 'own')), may hold values from 0 to 2047, as said below
- candidates: int32 [32, 262144], P(None, ('grp', 'own')), may hold values from 0 to 2047, as said below
- centroids: bfloat16 [2048, 1024], P('own'), may hold values from -3 to 3
- parents: int32 [2048, 1], replicated, may hold values from 0 to 255
Outputs:
- new_centroids: float32 [2048, 1024], P('own')
- top_centroids: float32 [256, 1024], replicated
- candidate_dist: float32 [32, 262144], P(None, ('grp', 'own'))
Inputs may be any that keep to these rules, and one draw needn't show every extreme that they name: `assign_one`: in each device's rows (aligned blocks of 1024 rows), at most 128 name a centroid of any one owner (ids o * 64 to (o + 1) * 64 - 1); one owner, the same in every block, is named by exactly 128. Each embedding's own level-one centroid (assign_one) is among its candidates. `parents`: every level-two id is named by some level-one centroid.
All inputs are finite; a program needn't handle non-finite values.
Results may differ from a plain program's by a relative error of at most 0.0003.
Values may be sent and summed in bfloat16 or wider, within the bound.
A program may use at most 64 MiB of HBM per device.

v0:
```python
import jax
import jax.numpy as jnp
from jax import lax
from jax.sharding import PartitionSpec as P

K2 = 256


def sent_to_all(array, axis):
    peers = lax.axis_size(axis)
    return lax.all_to_all(
        jnp.broadcast_to(array[None], (peers, *array.shape)), axis, 0, 0, tiled=True
    )


def taken_together(array, axis):
    return sent_to_all(array, axis).sum(axis=0)


def packed_total(arrays, axis):
    ends = [0]
    for a in arrays:
        ends.append(ends[-1] + a.size)
    subtotal = taken_together(jnp.concatenate([a.ravel() for a in arrays]), axis)
    return tuple((subtotal[b:e].reshape(a.shape) for a, b, e in zip(arrays, ends, ends[1:])))


def per_device(embeddings, assign_one, candidates, centroids, parents):
    row_count, feature_width = embeddings.shape
    owners = lax.axis_size("own")
    per_owner = centroids.shape[0]
    all_clusters = per_owner * owners
    cluster_ids = jnp.arange(all_clusters, dtype=jnp.int32)
    member = assign_one[None, :] == cluster_ids[:, None]
    partial_value = jnp.dot(
        member.astype(jnp.bfloat16), embeddings, preferred_element_type=jnp.float32
    )
    tallies = jnp.sum(member.astype(jnp.float32), axis=1)
    cluster_sums, counts = (
        lax.psum_scatter(partial_value, "own", scatter_dimension=0, tiled=True),
        lax.psum_scatter(tallies, "own", scatter_dimension=0, tiled=True),
    )
    cluster_sums, counts = packed_total((cluster_sums, counts), "grp")
    previous = centroids.astype(jnp.float32)
    new_centroids = jnp.where(
        counts[:, None] > 0, cluster_sums / jnp.maximum(counts, 1.0)[:, None], previous
    )
    row_norms = jnp.sum(jnp.square(embeddings.astype(jnp.float32)), axis=1)
    parent_ids = parents[:, 0]
    top_ids = jnp.arange(K2, dtype=jnp.int32)
    child_count = jnp.sum((parent_ids[None, :] == top_ids[:, None]).astype(jnp.float32), axis=1)
    piece = lax.all_gather(new_centroids, "own", axis=0, tiled=True)
    parent_hot = (top_ids[:, None] == parent_ids[None, :]).astype(jnp.float32)
    running = jnp.dot(
        parent_hot, piece, precision=lax.Precision.HIGHEST, preferred_element_type=jnp.float32
    )
    block_hat = piece.astype(jnp.bfloat16)
    count_rows = block_hat.shape[0]
    scores = lax.dot_general(
        block_hat, embeddings, (((1,), (1,)), ((), ())), preferred_element_type=jnp.float32
    )
    block_norms = jnp.sum(jnp.square(block_hat.astype(jnp.float32)), axis=1)
    all_dist = (row_norms[None, :] - 2.0 * scores + block_norms[:, None]) / feature_width
    grouped = candidates.reshape(-1, 8, candidates.shape[1])
    piece_ids = jnp.arange(count_rows, dtype=jnp.int32)

    def select_group(group_offsets):
        matches = group_offsets[:, None, :] == piece_ids[None, :, None]
        return jnp.sum(jnp.where(matches, all_dist[None, :, :], 0.0), axis=1)

    picked = lax.map(select_group, grouped).reshape(candidates.shape)
    top_centroids = running / child_count[:, None]
    return (new_centroids, top_centroids, picked)


def solution(mesh):
    in_specs = (
        P(("grp", "own"), None),
        P(("grp", "own")),
        P(None, ("grp", "own")),
        P("own", None),
        P(),
    )
    out_specs = (P("own", None), P(), P(None, ("grp", "own")))
    return jax.shard_map(
        per_device, mesh=mesh, in_specs=in_specs, out_specs=out_specs, check_vma=False
    )
```

profile of v0, /device:TPU:1, one launch (start us, length us, event | category | flops | bytes accessed | tf_op | source)
XLA Modules:
  0.0 300.2 jit_solution(12038653482316409246)
XLA Ops:
  7.2 0.0 reduce-scatter.2.cloned.1.call-start
  7.2 8.3 %fusion.2 = f32[2048,1024]{1,0:T(8,128)} fusion(bf16[1024,1024]{1,0:T(8,128)(2,1)} %param.7, s32[1024]{0:T(1024)} %param.8), kind=kOutput, calls=%fused_computation.9 | convolution fusion | flops 4297064448 | bytes 10489856 | tf_op jit(solution)/shard_map/dot_general | solution.py:35
  15.5 0.0 copy-start.5
  15.5 0.0 copy-start.4
  15.5 0.0 copy-start.2
  15.5 0.0 copy-start.3
  15.5 0.0 reduce-scatter.2.cloned.1.call-update
  15.5 0.0 all-gather.2.cloned.1.call-start
  15.6 0.6 copy-done.5
  16.2 0.6 dynamic-slice
  17.4 0.0 copy-done.4
  17.4 0.9 convert_reduce_fusion
  18.3 66.7 %all-reduce = f32[2048]{0:T(1024)S(1)} all-reduce(f32[2048]{0:T(1024)S(1)} %convert_reduce_fusion), channel_id=3, replica_groups=mesh['grp'=8,'own'=32] {'own'}, use_global_device_ids=true, to_apply=%region_2.0.clone | all-reduce | flops 2048 | bytes 16384
  85.0 0.1 dynamic-slice.1
  85.1 32.9 %reduce-scatter.2.cloned.1.call-done = f32[64,1024]{1,0:T(8,128)} async-done(((f32[2048,1024]{1,0:T(8,128)}), f32[64,1024]{1,0:T(8,128)}) %reduce-scatter.2.cloned.1.call-update) | async-done | bytes 262160 | tf_op jit(solution)/shard_map/reduce_scatter | solution.py:40
  118.1 1.0 copy.12
  119.1 1.1 broadcast_in_dim.23
  120.2 54.7 %all_to_all.6 = f32[8,1,65600]{2,1,0:T(1,128)S(1)} all-to-all(f32[8,1,65600]{2,1,0:T(1,128)S(1)} %broadcast_in_dim.23), channel_id=1, replica_groups=mesh['grp'=8,'own'=32] {'grp'}, dimensions={0} | all-to-all | bytes 4198400 | tf_op jit(solution)/shard_map/all_to_all | solution.py:11
  174.9 1.5 reduce_sum.55
  176.4 0.0 copy-start.1
  176.5 0.0 copy-done.2
  176.5 0.8 convert_select_fusion
  177.3 0.0 all-gather.2.cloned.1.call-update
  177.4 0.0 copy-done.3
  177.4 0.3 convert_reduce_fusion.1
  177.7 2.1 multiply_reduce_fusion.1
  179.7 53.4 %all-gather.2.cloned.1.call-done = f32[2048,1024]{1,0:T(8,128)} async-done(((f32[64,1024]{1,0:T(8,128)}), f32[2048,1024]{1,0:T(8,128)}) %all-gather.2.cloned.1.call-update) | async-done | bytes 8388624 | tf_op jit(solution)/shard_map/all_gather | solution.py:52
  233.2 0.0 copy-start
  233.2 4.1 %multiply_reduce_fusion = f32[2048]{0:T(1024)S(1)} fusion(f32[2048,1024]{1,0:T(8,128)} %all-gather.2.cloned.1.call-done), kind=kLoop, calls=%fused_computation.6 | loop fusion | flops 8386560 | bytes 8396800 | tf_op jit(solution)/shard_map/reduce_sum | solution.py:62
  237.3 0.0 copy-done.1
  237.3 1.6 copy-done
  238.9 7.4 %add_multiply_fusion = f32[2048,1024]{1,0:T(8,128)} fusion(bf16[1024,1024]{1,0:T(8,128)(2,1)S(1)} %copy-done.1, f32[2048]{0:T(1024)S(1)} %multiply_reduce_fusion, f32[1024]{0:T(1024)S(1)} %multiply_reduce_fusion.1, f32[2048,1024]{1,0:T(8,128)S(1)} %copy-done), kind=kOutput, calls=%fused_computation.5 | convolution fusion | flops 4305453056 | bytes 18886656 | tf_op jit(solution)/shard_map/dot_general | solution.py:59
  246.4 39.1 %while.11 = (s32[]{:T(128)}, f32[4,8,1024]{2,1,0:T(8,128)}, s32[4,8,1024]{2,1,0:T(8,128)}, f32[2048,1024]{1,0:T(8,128)}, s32[]{:T(128)}) while((s32[]{:T(128)}, f32[4,8,1024]{2,1,0:T(8,128)}, s32[4,8,1024]{2,1,0:T(8,128)}, f32[2048,1024]{1,0:T(8,128)}, s32[]{:T(128)}) %tuple.32), condition=%wide.region_9.10_spmd.clone, body=%wide.region_7.9_spmd.clone.sunk | while | flops 50323456 | bytes 8585793 | solution.py:71
  246.4 0.8 dynamic-slice_bitcast_fusion.2
  247.1 8.4 %select_reduce_fusion.2 = f32[8,1024]{1,0:T(8,128)S(1)} fusion(f32[2048,1024]{1,0:T(8,128)} %get-tuple-element.87, s32[8,1024]{1,0:T(8,128)S(1)} %dynamic-slice_bitcast_fusion.2), kind=kLoop, calls=%fused_computation.2.clone.1 | loop fusion | flops 50323456 | bytes 8454144 | tf_op jit(solution)/shard_map/while/body/eval_jaxpr/reduce_sum | solution.py:69
  255.5 0.6 bitcast_dynamic-update-slice_fusion.2
  256.1 0.8 dynamic-slice_bitcast_fusion.2
  256.9 8.4 %select_reduce_fusion.2 = f32[8,1024]{1,0:T(8,128)S(1)} fusion(f32[2048,1024]{1,0:T(8,128)} %get-tuple-element.87, s32[8,1024]{1,0:T(8,128)S(1)} %dynamic-slice_bitcast_fusion.2), kind=kLoop, calls=%fused_computation.2.clone.1 | loop fusion | flops 50323456 | bytes 8454144 | tf_op jit(solution)/shard_map/while/body/eval_jaxpr/reduce_sum | solution.py:69
  265.3 0.6 bitcast_dynamic-update-slice_fusion.2
  265.9 0.8 dynamic-slice_bitcast_fusion.2
  266.7 8.4 %select_reduce_fusion.2 = f32[8,1024]{1,0:T(8,128)S(1)} fusion(f32[2048,1024]{1,0:T(8,128)} %get-tuple-element.87, s32[8,1024]{1,0:T(8,128)S(1)} %dynamic-slice_bitcast_fusion.2), kind=kLoop, calls=%fused_computation.2.clone.1 | loop fusion | flops 50323456 | bytes 8454144 | tf_op jit(solution)/shard_map/while/body/eval_jaxpr/reduce_sum | solution.py:69
  275.0 0.6 bitcast_dynamic-update-slice_fusion.2
  275.7 0.8 dynamic-slice_bitcast_fusion.2
  276.4 8.4 %select_reduce_fusion.2 = f32[8,1024]{1,0:T(8,128)S(1)} fusion(f32[2048,1024]{1,0:T(8,128)} %get-tuple-element.87, s32[8,1024]{1,0:T(8,128)S(1)} %dynamic-slice_bitcast_fusion.2), kind=kLoop, calls=%fused_computation.2.clone.1 | loop fusion | flops 50323456 | bytes 8454144 | tf_op jit(solution)/shard_map/while/body/eval_jaxpr/reduce_sum | solution.py:69
  284.8 0.6 bitcast_dynamic-update-slice_fusion.2
  285.4 7.9 %fusion.6 = f32[256,1024]{1,0:T(8,128)} fusion(f32[2048,1024]{1,0:T(8,128)} %all-gather.2.cloned.1.call-done, s32[2048]{0:T(1024)S(1)} %bitcast.21, f32[256]{0:T(256)S(1)} %convert_reduce_fusion.1), kind=kOutput, calls=%fused_computation.17 | convolution fusion | flops 6443237376 | bytes 9446400 | tf_op jit(solution)/shard_map/dot_general | solution.py:54
  (6 shorter events, 0.1 us)
Async XLA Ops:
  7.2 110.9 %reduce-scatter.2.cloned.1.call-start = ((), (), s32[]{:S(2)}) async-start(), calls=%async_computation.2 | async-start | bytes 8650752 | tf_op jit(solution)/shard_map/reduce_scatter | solution.py:40
  15.5 0.7 copy-start.5
  15.5 1.9 copy-start.4
  15.5 161.0 %copy-start.2 = (bf16[64,1024]{1,0:T(8,128)(2,1)S(1)}, bf16[64,1024]{1,0:T(8,128)(2,1)}, u32[]{:S(2)}) copy-start(bf16[64,1024]{1,0:T(8,128)(2,1)} %param.10) | copy-start | bytes 393220
  15.5 161.9 %copy-start.3 = (s32[2048,1]{0,1:T(1,128)S(1)}, s32[2048,1]{0,1:T(1,128)}, u32[]{:S(2)}) copy-start(s32[2048,1]{0,1:T(1,128)} %param.11) | copy-start | bytes 24580
  15.5 217.7 %all-gather.2.cloned.1.call-start = ((), (), s32[]{:S(2)}) async-start(), calls=%async_computation.3 | async-start | bytes 8650752 | tf_op jit(solution)/shard_map/all_gather | solution.py:52
  176.4 60.9 %copy-start.1 = (bf16[1024,1024]{1,0:T(8,128)(2,1)S(1)}, bf16[1024,1024]{1,0:T(8,128)(2,1)}, u32[]{:S(2)}) copy-start(bf16[1024,1024]{1,0:T(8,128)(2,1)} %param.7) | copy-start | bytes 6291460
  233.2 5.8 %copy-start = (f32[2048,1024]{1,0:T(8,128)S(1)}, f32[2048,1024]{1,0:T(8,128)}, u32[]{:S(2)}) copy-start(f32[2048,1024]{1,0:T(8,128)} %all-gather.2.cloned.1.call-done) | copy-start | bytes 25165828
Sparse Core Ops, SparseCore 0:
  15.6 102.3 reduce-scatter.1
  177.5 55.6 all-gather.1
where the time goes:
time: 301 us; the launch traced here: 300 us
  blocking collectives  121 us (40%)
  waiting for transfers between devices  86.4 us (29%)
  other arithmetic  43.3 us (14%)
  matrix products  23.6 us (8%)
  between operations  14.8 us (5%)
  local copies, waits for them, and re-layouts  10.6 us (4%)
    unnamed x1, blocking collectives  66.7 us
    all_to_all x1, blocking collectives, sent_to_all(): lax.all_to_all(jnp.broadcast_to(array[None], (peers, *array.shape)), axis...  54.7 us
    all_gather x1, waiting for transfers between devices, per_device(): piece = lax.all_gather(new_centroids, 'own', axis=0, tiled=True)  53.4 us
    reduce_sum x4, other arithmetic, select_group(): return jnp.sum(jnp.where(matches, all_dist[None, :, :], 0.0), axis=1)  33.5 us
    reduce_scatter x1, waiting for transfers between devices, per_device(): lax.psum_scatter(partial_value, 'own', scatter_dimension=0, tiled=True)  32.9 us
    dot_general x1, matrix products, per_device(): jnp.dot(member.astype(jnp.bfloat16), embeddings, preferred_element_type=j...  8.27 us
    dot_general x1, matrix products, per_device(): jnp.dot(parent_hot, piece, precision=lax.Precision.HIGHEST, preferred_ele...  7.94 us
    dot_general x1, matrix products, per_device(): lax.dot_general(block_hat, embeddings, (((1,), (1,)), ((), ())), preferre...  7.41 us
  transfers between devices with their start and end apart: 2, of which 2 were waited for; matrix products, arithmetic and copies ran while one was open for 1% of the time, Pallas kernels for 0%

commit v1 on v0

v1 whole, which is shorter than its diff:
```python
import functools

import jax
import jax.numpy as jnp
from jax import lax
from jax.experimental import pallas as pl
from jax.experimental.pallas import tpu as pltpu
from jax.sharding import PartitionSpec as P

MESH = pl.DeviceIdType.MESH
NT = (((1,), (1,)), ((), ()))
NX, NY, NZ = 4, 4, 8
D = 1024
W = D + 128
ROWS = 1024
K1 = 2048
K2 = 256
NCAND = 32


def encode(x):
    top = jnp.max(jnp.abs(x), axis=1, keepdims=True)
    t = jnp.ceil(jnp.log2(jnp.maximum(top, 1e-30) * (1.0 / 32700.0)) * 256.0)
    t = jnp.maximum(t, -30000.0)
    codes = jnp.round(x * jnp.exp2(t * (-1.0 / 256.0))).astype(jnp.int32).astype(jnp.int16)
    scale = jnp.broadcast_to(t, (x.shape[0], 128)).astype(jnp.int32).astype(jnp.int16)
    return codes, scale


def decode(block):
    wide = block.astype(jnp.int32).astype(jnp.float32)
    s = jnp.exp2(wide[:, D:] * (1.0 / 256.0))
    return jnp.concatenate([wide[:, j * 128 : (j + 1) * 128] * s for j in range(D // 128)], axis=1)


def exchange_kernel(
    emb, ids_ref, cent_ref, gathered,
    rows_buf, ids_far, part, own, cnt, cnt_in, s1, r1, s2, r2, zs, zr, mine,
    local_sem, send, recv, gsend, grecv,
):
    z = lax.axis_index("grp")
    o = lax.axis_index("own")
    c = lax.rem(o, 2)
    x = lax.rem(lax.div(o, 2), NX)
    y = lax.div(o, 2 * NX)

    def at(dx=0, dy=0, dz=0, flip=False):
        xx = lax.rem(x + dx + NX, NX)
        yy = lax.rem(y + dy + NY, NY)
        zz = lax.rem(z + dz + NZ, NZ)
        cc = 1 - c if flip else c
        return (zz, (yy * NX + xx) * 2 + cc)

    def along(axis, step):
        return at(dx=step) if axis == 0 else at(dy=step)

    peers = [at(flip=True)]
    peers += [at(dx=j) for j in (1, 2, 3)]
    peers += [at(dy=j) for j in (1, 2, 3)]
    peers += [at(dz=j) for j in range(1, NZ)]

    fetch = pltpu.make_async_copy(emb, rows_buf.at[pl.ds(0, ROWS)], local_sem.at[0])
    fetch.start()

    barrier = pltpu.get_barrier_semaphore()
    for peer in peers:
        pl.semaphore_signal(barrier, inc=1, device_id=peer, device_id_type=MESH)
    pl.semaphore_wait(barrier, len(peers))

    used = [0]

    def copy(src, dst, to):
        i = used[0]
        used[0] += 1
        return pltpu.make_async_remote_copy(
            src_ref=src, dst_ref=dst, send_sem=send.at[i], recv_sem=recv.at[i], device_id=to, device_id_type=MESH
        )

    sent = []

    def go(m):
        m.start()
        sent.append(m)
        return m

    far_ids = go(copy(ids_ref, ids_far, at(flip=True)))
    far = [
        go(copy(emb.at[pl.ds(q * 256, 256)], rows_buf.at[pl.ds(ROWS + q * 256, 256)], at(flip=True)))
        for q in range(4)
    ]

    place = (2, 1, 3, 0)

    def cluster_ids(g):
        r = lax.broadcasted_iota(jnp.int32, (256, 1), 0)
        k = lax.rem(lax.div(r, 32), 4)
        i = lax.rem(r, 32)
        xg = lax.rem(x + place[g], NX)
        yg = lax.rem(y + place[g], NY)
        first = ((k * NX + xg) * 2 + c) * 64 + i
        second = ((yg * NX + k) * 2 + c) * 64 + 32 + i
        return jnp.where(r < 128, first, second)

    def hot(g, ids):
        return jnp.where(ids[...] == cluster_ids(g), 1.0, 0.0).astype(jnp.bfloat16)

    ones = jnp.ones((8, ROWS), jnp.bfloat16)

    def tally(h):
        return lax.dot_general(ones, h, NT, preferred_element_type=jnp.float32)[0:1]

    fetch.wait()
    near = []
    for g in range(4):
        h = hot(g, ids_ref)
        near.append(tally(h))
        part[g] = jnp.dot(h, rows_buf[0:ROWS], preferred_element_type=jnp.float32)

    far_ids.wait_recv()
    for m in far:
        m.wait_recv()

    def pack(value_of, buf, rows):
        @pl.loop(0, rows // 16)
        def _(b):
            i = pl.multiple_of(b * 16, 16)
            codes, scale = encode(value_of(i))
            buf[pl.ds(i, 16), 0:D] = codes
            buf[pl.ds(i, 16), D:W] = scale

    msgs = {}
    for g in range(4):
        h = hot(g, ids_far)
        both = near[g] + tally(h)
        xg = lax.rem(x + place[g], NX)
        yg = lax.rem(y + place[g], NY)
        cnt[0, pl.ds(xg, 1)] = both[:, 0:128]
        cnt[0, pl.ds(4 + yg, 1)] = both[:, 128:256]
        part[g] += jnp.dot(h, rows_buf[ROWS : 2 * ROWS], preferred_element_type=jnp.float32)
        if g == 0:
            for colour in range(2):
                for d in range(2):
                    pack(lambda i: part[0, pl.ds(colour * 128 + d * 64 + i, 16)], s1.at[colour, d, 0], 64)
                    msgs[colour, d, 0] = go(copy(s1.at[colour, d, 0], r1.at[colour, d, 0], along(colour, 1 - 2 * d)))
        elif g < 3:
            d = g - 1
            for colour in range(2):
                pack(lambda i: part[g, pl.ds(colour * 128 + (1 - d) * 64 + i, 16)], s1.at[colour, d, 1], 64)
                msgs[colour, d, 1] = go(copy(s1.at[colour, d, 1], r1.at[colour, d, 1], along(colour, 1 - 2 * d)))

    cnt_x = [go(copy(cnt.at[0], cnt_in.at[j - 1], at(dx=j))) for j in (1, 2, 3)]

    for colour in range(2):
        for d in range(2):
            msgs[colour, d, 0].wait_recv()
            pack(
                lambda i: part[1 + d, pl.ds(colour * 128 + d * 64 + i, 16)] + decode(r1[colour, d, 0, pl.ds(i, 16)]),
                s1.at[colour, d, 2],
                64,
            )
            msgs[colour, d, 2] = go(copy(s1.at[colour, d, 2], r1.at[colour, d, 2], along(colour, 1 - 2 * d)))

    for m in cnt_x:
        m.wait_recv()
    cnt[1] = cnt[0] + cnt_in[0] + cnt_in[1] + cnt_in[2]
    cnt_y = [go(copy(cnt.at[1], cnt_in.at[2 + j], at(dy=j))) for j in (1, 2, 3)]

    for colour in range(2):
        for d in range(2):
            msgs[colour, d, 1].wait_recv()
    for colour in range(2):
        for d in range(2):
            msgs[colour, d, 2].wait_recv()

    @pl.loop(0, 8)
    def _(b):
        i = pl.multiple_of(b * 16, 16)
        for colour in range(2):
            v = part[3, pl.ds(colour * 128 + i, 16)]
            own[colour, pl.ds(i, 16)] = v

    for colour in range(2):
        for d in range(2):
            for kind, half in ((1, 1 - d), (2, d)):

                @pl.loop(0, 4)
                def _(b):
                    i = pl.multiple_of(b * 16, 16)
                    own[colour, pl.ds(half * 64 + i, 16)] += decode(r1[colour, d, kind, pl.ds(i, 16)])

    def seg(colour, step, half):
        along_other = y if colour == 0 else x
        k = lax.rem(along_other + step, 4)
        return pl.ds(pl.multiple_of(k * 32 + half * 16, 16), 16)

    m2 = {}
    for colour in range(2):
        axis = 1 - colour
        for d in range(2):
            pack(lambda i: own[colour, seg(colour, 2, d)], s2.at[colour, d, 0], 16)
            m2[colour, d, 0] = go(copy(s2.at[colour, d, 0], r2.at[colour, d, 0], along(axis, 1 - 2 * d)))
    for colour in range(2):
        axis = 1 - colour
        for d in range(2):
            pack(lambda i: own[colour, seg(colour, place[1 + d], 1 - d)], s2.at[colour, d, 1], 16)
            m2[colour, d, 1] = go(copy(s2.at[colour, d, 1], r2.at[colour, d, 1], along(axis, 1 - 2 * d)))
    for m in cnt_y:
        m.wait_recv()
    cnt[2] = cnt[1] + cnt_in[3] + cnt_in[4] + cnt_in[5]
    cnt_z = [go(copy(cnt.at[2], cnt_in.at[5 + j], at(dz=j))) for j in range(1, NZ)]
    for colour in range(2):
        axis = 1 - colour
        for d in range(2):
            m2[colour, d, 0].wait_recv()
            pack(
                lambda i: own[colour, seg(colour, place[1 + d], d)] + decode(r2[colour, d, 0]),
                s2.at[colour, d, 2],
                16,
            )
            m2[colour, d, 2] = go(copy(s2.at[colour, d, 2], r2.at[colour, d, 2], along(axis, 1 - 2 * d)))
    for colour in range(2):
        for d in range(2):
            m2[colour, d, 1].wait_recv()
            m2[colour, d, 2].wait_recv()
    for colour in range(2):
        for half in range(2):
            total = (
                own[colour, seg(colour, 0, half)]
                + decode(r2[colour, half, 2])
                + decode(r2[colour, 1 - half, 1])
            )
            base = colour * 32 + half * 16
            part[0, pl.ds(base, 16)] = total
            codes, scale = encode(total)
            for q in range(2):
                b = base // 8 + q
                zs[b, :, 0:D] = codes[q * 8 : q * 8 + 8]
                zs[b, :, D:W] = scale[q * 8 : q * 8 + 8]

    m3 = [go(copy(zs.at[lax.rem(z + j, NZ)], zr.at[j - 1], at(dz=j))) for j in range(1, NZ)]
    for m in cnt_z:
        m.wait_recv()
    count_sum = cnt[2]
    for j in range(1, NZ):
        count_sum += cnt_in[5 + j]
    cnt[3] = count_sum
    low = z < 4
    crow = jnp.where(low, x, 4 + y)
    cbase = jnp.where(low, y, x) * 32 + lax.rem(z, 4) * 8
    line = cnt[3, pl.ds(crow, 1)]
    lane = lax.broadcasted_iota(jnp.int32, (8, 128), 1)
    sub = lax.broadcasted_iota(jnp.int32, (8, 128), 0)
    counts = jnp.sum(jnp.where(lane == cbase + sub, jnp.broadcast_to(line, (8, 128)), 0.0), axis=1, keepdims=True)
    first = pl.multiple_of(z * 8, 8)
    total = part[0, pl.ds(first, 8)]
    for m, j in zip(m3, range(1, NZ)):
        m.wait_recv()
        total += decode(zr[j - 1])
    previous = cent_ref[pl.ds(first, 8)].astype(jnp.float32)
    new = jnp.where(counts > 0, total / jnp.maximum(counts, 1.0), previous)
    codes, scale = encode(new)
    mine[:, 0:D] = codes
    mine[:, D:W] = scale

    used_g = [0]

    def gcopy(ref, to, src=None):
        i = used_g[0]
        used_g[0] += 1
        return pltpu.make_async_remote_copy(
            src_ref=ref if src is None else src, dst_ref=ref,
            send_sem=gsend.at[i], recv_sem=grecv.at[i], device_id=to, device_id_type=MESH,
        )

    here = gathered.at[y, x, c, z]
    keep = pltpu.make_async_copy(mine, here, local_sem.at[1])
    keep.start()
    mz = [go(gcopy(here, at(dz=j), src=mine)) for j in range(1, NZ)]
    keep.wait()
    for m in mz:
        m.wait_recv()

    def block(colour, far1, far2, lo=0, n=4):
        a, b = lax.rem(y + (far1 if colour == 0 else far2), 4), lax.rem(x + (far2 if colour == 0 else far1), 4)
        return gathered.at[a, b, c, pl.ds(colour * 4 + lo, n)]

    to_core = []

    def share(ref):
        to_core.append(go(gcopy(ref, at(flip=True))))

    def first_axis(colour, d):
        return along(1 - colour, 1 - 2 * d)

    def second_axis(colour, d):
        return along(colour, 1 - 2 * d)

    step_a = {}
    step_b = {}
    for colour in range(2):
        for d in range(2):
            step_a[colour, d] = go(gcopy(block(colour, 0, 0), first_axis(colour, d)))
    for colour in range(2):
        for d in range(2):
            step_b[colour, 0, d] = go(gcopy(block(colour, 0, 0), second_axis(colour, d)))
    for colour in range(2):
        share(block(colour, 0, 0))
    origin = (3, 1)
    relay_a = {}
    for colour in range(2):
        for d in range(2):
            step_a[colour, d].wait_recv()
            relay_a[colour, d] = go(gcopy(block(colour, origin[d], 0, 2 * d, 2), first_axis(colour, d)))
    for colour in range(2):
        for d in range(2):
            for e in range(2):
                step_b[colour, origin[d], e] = go(gcopy(block(colour, origin[d], 0), second_axis(colour, e)))
            share(block(colour, origin[d], 0))
    relay_b = {}

    def arrived(colour, k):
        for e in range(2):
            step_b[colour, k, e].wait_recv()
            relay_b[colour, k, e] = go(gcopy(block(colour, k, origin[e], 2 * e, 2), second_axis(colour, e)))
            share(block(colour, k, origin[e]))

    for colour in range(2):
        arrived(colour, 0)
    for colour in range(2):
        for d in range(2):
            relay_a[colour, d].wait_recv()
        for e in range(2):
            step_b[colour, 2, e] = go(gcopy(block(colour, 2, 0), second_axis(colour, e)))
        share(block(colour, 2, 0))
    for k in (3, 1, 2):
        for colour in range(2):
            arrived(colour, k)
    for k in (0, 3, 1, 2):
        for colour in range(2):
            for e in range(2):
                relay_b[colour, k, e].wait_recv()
            share(block(colour, k, 2))
    for m in to_core:
        m.wait_recv()
    for m in sent:
        m.wait_send()


N_SEND = 60
N_GATHER = 100


def exchange(emb, ids, centroids):
    vmem = pl.BlockSpec(memory_space=pltpu.VMEM)
    hbm = pl.BlockSpec(memory_space=pl.ANY)
    i16 = jnp.int16
    return pl.pallas_call(
        exchange_kernel,
        out_shape=jax.ShapeDtypeStruct((NY, NX, 2, NZ, 8, W), i16),
        in_specs=[hbm, vmem, vmem],
        out_specs=hbm,
        scratch_shapes=[
            pltpu.VMEM((2 * ROWS, D), jnp.bfloat16),
            pltpu.VMEM((1, ROWS), jnp.int32),
            pltpu.VMEM((4, 256, D), jnp.float32),
            pltpu.VMEM((2, 128, D), jnp.float32),
            pltpu.VMEM((4, 8, 128), jnp.float32),
            pltpu.VMEM((13, 8, 128), jnp.float32),
            pltpu.VMEM((2, 2, 3, 64, W), i16),
            pltpu.VMEM((2, 2, 3, 64, W), i16),
            pltpu.VMEM((2, 2, 3, 16, W), i16),
            pltpu.VMEM((2, 2, 3, 16, W), i16),
            pltpu.VMEM((8, 8, W), i16),
            pltpu.VMEM((7, 8, W), i16),
            pltpu.VMEM((8, W), i16),
            pltpu.SemaphoreType.DMA((2,)),
            pltpu.SemaphoreType.DMA((N_SEND,)),
            pltpu.SemaphoreType.DMA((N_SEND,)),
            pltpu.SemaphoreType.DMA((N_GATHER,)),
            pltpu.SemaphoreType.DMA((N_GATHER,)),
        ],
        compiler_params=pltpu.CompilerParams(collective_id=0, has_side_effects=True, vmem_limit_bytes=48 << 20),
    )(emb, ids, centroids)


TILE = 256


def local_kernel(emb, cand, codes, parents, dist, top, new, rounded, norms):
    @pl.when(pl.program_id(0) == 0)
    def _():
        first = pl.multiple_of(lax.axis_index("own") * 64, 64)
        new[...] = decode(codes[pl.ds(first, 64)])
        top[...] = jnp.zeros_like(top)

        def chunk(b, children):
            i = pl.multiple_of(b * 256, 256)
            value = decode(codes[pl.ds(i, 256)])
            near = value.astype(jnp.bfloat16)
            wide = near.astype(jnp.float32)
            rest = (value - wide).astype(jnp.bfloat16)
            rounded[pl.ds(i, 256)] = near
            squares = jnp.zeros((256, 128), jnp.float32)
            for j in range(D // 128):
                v = wide[:, j * 128 : (j + 1) * 128]
                squares += v * v
            norms[:, pl.ds(i, 256)] = lax.dot_general(
                jnp.ones((8, 128), jnp.float32), squares, NT,
                precision=lax.Precision.HIGHEST, preferred_element_type=jnp.float32,
            )
            hot = jnp.where(
                parents[:, pl.ds(i, 256)] == lax.broadcasted_iota(jnp.int32, (K2, 256), 0), 1.0, 0.0
            )
            h = hot.astype(jnp.bfloat16)
            top[...] += jnp.dot(h, near, preferred_element_type=jnp.float32) + jnp.dot(
                h, rest, preferred_element_type=jnp.float32
            )
            return children + jnp.sum(hot, axis=1, keepdims=True)

        children = lax.fori_loop(0, K1 // 256, chunk, jnp.zeros((K2, 1), jnp.float32))
        top[...] = top[...] / children

    e = emb[...]
    wide = e.astype(jnp.float32)
    own_norm = jnp.sum(wide * wide, axis=1, keepdims=True)
    ids = jnp.concatenate([cand[...], jnp.zeros((128 - NCAND, TILE), jnp.int32)], axis=0)
    ids = jnp.concatenate([ids[:, q * 128 : (q + 1) * 128].T for q in range(TILE // 128)], axis=0)
    low = ids & 127
    high = ids >> 7
    acc = jnp.zeros((TILE, 128), jnp.float32)
    for b in range(K1 // 256):
        s = lax.dot_general(e, rounded[b * 256 : (b + 1) * 256], NT, preferred_element_type=jnp.float32)
        s = norms[0:1, b * 256 : (b + 1) * 256] - 2.0 * s
        for q in range(2):
            g = jnp.take_along_axis(s[:, q * 128 : (q + 1) * 128], low, axis=1, mode="promise_in_bounds")
            acc = jnp.where(high == 2 * b + q, g, acc)
    acc = (acc + own_norm) * (1.0 / D)
    dist[...] = jnp.concatenate([acc[q * 128 : (q + 1) * 128].T[0:NCAND] for q in range(TILE // 128)], axis=1)


def local(emb, cand, codes, parents):
    whole = lambda *shape: pl.BlockSpec(shape, lambda i: (0, 0), pipeline_mode=pl.Buffered(1))
    f32 = jnp.float32
    return pl.pallas_call(
        local_kernel,
        grid=(ROWS // TILE,),
        in_specs=[
            pl.BlockSpec((TILE, D), lambda i: (i, 0)),
            pl.BlockSpec((NCAND, TILE), lambda i: (0, i)),
            whole(K1, W),
            whole(1, K1),
        ],
        out_specs=[pl.BlockSpec((NCAND, TILE), lambda i: (0, i)), whole(K2, D), whole(64, D)],
        out_shape=[
            jax.ShapeDtypeStruct((NCAND, ROWS), f32),
            jax.ShapeDtypeStruct((K2, D), f32),
            jax.ShapeDtypeStruct((64, D), f32),
        ],
        scratch_shapes=[pltpu.VMEM((K1, D), jnp.bfloat16), pltpu.VMEM((8, K1), f32)],
        compiler_params=pltpu.CompilerParams(vmem_limit_bytes=48 << 20),
    )(emb, cand, codes, parents)


def per_device(embeddings, assign_one, candidates, centroids, parents):
    codes = exchange(embeddings, assign_one.reshape(1, ROWS), centroids)
    dist, top, new = local(embeddings, candidates, codes.reshape(K1, W), parents.reshape(1, K1))
    return new, top, dist


def solution(mesh):
    both = ("grp", "own")
    return jax.shard_map(
        per_device,
        mesh=mesh,
        in_specs=(P(both, None), P(both), P(None, both), P("own", None), P()),
        out_specs=(P("own", None), P(), P(None, both)),
        check_vma=False,
    )
```

time: 301 us -> 91.8 us (0.30)
  blocking collectives: 121 us -> 0 us
  Pallas kernels: 0 us -> 87.8 us
  waiting for transfers between devices: 86.4 us -> 0 us
  other arithmetic: 43.3 us -> 0 us
  matrix products: 23.6 us -> 0 us
  between operations: 14.8 us -> 0.67 us
  local copies, waits for them, and re-layouts: 10.6 us -> 3.18 us
    pallas_call x0 -> x2, Pallas kernels: none -> 87.8 us  [the longest x1 71.5 us: exchange(): pl.pallas_call(exchange_kernel, out_shape=jax.ShapeDtypeStruct((NY, NX, 2...]
    unnamed x1 -> x0, blocking collectives: 66.7 us -> none
    all_to_all x1 -> x0, blocking collectives: 54.7 us -> none  [sent_to_all(): lax.all_to_all(jnp.broadcast_to(array[None], (peers, *array.shape)), axis...]
    all_gather x1 -> x0, waiting for transfers between devices: 53.4 us -> none  [per_device(): piece = lax.all_gather(new_centroids, 'own', axis=0, tiled=True)]
    reduce_sum x9 -> x0, other arithmetic: 42.4 us -> none  [the longest x4 33.5 us: select_group(): return jnp.sum(jnp.where(matches, all_dist[None, :, :], 0.0), axis=1)]
    reduce_scatter x1 -> x0, waiting for transfers between devices: 32.9 us -> none  [per_device(): lax.psum_scatter(partial_value, 'own', scatter_dimension=0, tiled=True)]
    dot_general x3 -> x0, matrix products: 23.6 us -> none  [the longest x1 8.27 us: per_device(): jnp.dot(member.astype(jnp.bfloat16), embeddings, preferred_element_type=j...]
    eq x4 -> x0, local copies, waits for them, and re-layouts: 3.04 us -> none  [select_group(): matches = group_offsets[:, None, :] == piece_ids[None, :, None]]
  transfers between devices with their start and end apart: 2 -> 0, of which waited for: 2 -> 0; matrix products, arithmetic and copies ran while one was open for 1% -> 0% of each run, Pallas kernels for 0% -> 0%
where the time goes in v1:
time: 91.8 us; the launch traced here: 91.6 us
  Pallas kernels  87.8 us (96%)
  local copies, waits for them, and re-layouts  3.18 us (3%)
    pallas_call x1, Pallas kernels, exchange(): pl.pallas_call(exchange_kernel, out_shape=jax.ShapeDtypeStruct((NY, NX, 2...  71.5 us
    pallas_call x1, Pallas kernels, local(): pl.pallas_call(local_kernel, grid=(ROWS // TILE,), in_specs=[pl.BlockSpec...  16.2 us
    unnamed x10, local copies, waits for them, and re-layouts  3.18 us

profile of v1, /device:TPU:1, one launch (start us, length us, event | category | flops | bytes accessed | tf_op | source)
XLA Modules:
  0.0 91.6 jit_solution(8815294638892306185)
XLA Ops:
  0.6 0.0 copy-start
  0.6 1.6 %copy-done = bf16[1024,1024]{1,0:T(8,128)(2,1)S(1)} copy-done((bf16[1024,1024]{1,0:T(8,128)(2,1)S(1)}, bf16[1024,1024]{1,0:T(8,128)(2,1)}, u32[]{:S(2)}) %copy-start) | copy-done | bytes 2097176
  2.2 0.0 copy-start.1
  2.2 0.9 copy-done.1
  3.1 0.0 copy-start.4
  3.1 0.7 copy-done.4
  3.8 0.0 copy-start.2
  3.8 0.0 copy-start.3
  3.8 71.5 %shard_map.76 = s16[4,4,2,8,8,1152]{5,4,3,2,1,0:T(8,128)(2,1)} custom-call(bf16[1024,1024]{1,0:T(8,128)(2,1)S(1)} %copy-done, s32[1,1024]{1,0:T(1,128)S(1)} %bitcast.4, bf16[64,1024]{1,0:T(8,128)(2,1)S(1)} %copy-done.1), custom_call_target="tpu_custom_call" | custom-call | tf_op jit(solution)/shard_map/pallas_call | solution.py:357
  75.3 0.0 copy-done.2
  75.3 0.0 copy-done.3
  75.4 16.2 %shard_map.77 = (f32[32,1024]{1,0:T(8,128)}, f32[256,1024]{1,0:T(8,128)}, f32[64,1024]{1,0:T(8,128)}) custom-call(bf16[1024,1024]{1,0:T(8,128)(2,1)S(1)} %copy-done, s32[32,1024]{1,0:T(8,128)S(1)} %copy-done.2, s16[2048,1152]{1,0:T(8,128)(2,1)} %bitcast.5, s32[1,2048]{1,0:T(1,128)S(1)} %bitcast.3), custom_call_target="tpu_custom_call" | custom-call | tf_op jit(solution)/shard_map/pallas_call | solution.py:444
Async XLA Ops:
  0.6 1.6 %copy-start = (bf16[1024,1024]{1,0:T(8,128)(2,1)S(1)}, bf16[1024,1024]{1,0:T(8,128)(2,1)}, u32[]{:S(2)}) copy-start(bf16[1024,1024]{1,0:T(8,128)(2,1)} %emb.3) | copy-start | bytes 6291460
  2.2 0.9 copy-start.1
  3.1 0.7 copy-start.4
  3.8 71.5 %copy-start.2 = (s32[32,1024]{1,0:T(8,128)S(1)}, s32[32,1024]{1,0:T(8,128)}, u32[]{:S(2)}) copy-start(s32[32,1024]{1,0:T(8,128)} %cand.1) | copy-start | bytes 393220
  3.8 71.5 %copy-start.3 = (s32[2048,1]{0,1:T(1,128)S(1)}, s32[2048,1]{0,1:T(1,128)}, u32[]{:S(2)}) copy-start(s32[2048,1]{0,1:T(1,128)} %param.9) | copy-start | bytes 24580
